TPU v7x, 128 devices: a whole 4x4x4 slice. The times are simulated.
128 devices in a mesh: row: 8 (over y, core), col: 16 (over z, x).
Axes of the slice: x: 4, y: 4, z: 4, core: 2. Of those that a mesh axis runs over, the one named last changes fastest.
Arguments:
- chol_window: bfloat16 [48, 48, 1536], P(None, None, ('row', 'col')), may hold values from -0.3125 to 0.3125
- chol_pairs: bfloat16 [512, 512, 1536], P('row', 'col'), may hold values from -0.3125 to 0.3125
- amplitudes: bfloat16 [48, 512, 1024], P(None, 'col', 'row'), may hold values from -6 to 6
- eps_window: float32 [48], P('col'), may hold values from 0.5 to 2
- eps_virtual: float32 [512], P('row'), may hold values from 0.5 to 2
- eps_occupied: float32 [1024], replicated, may hold values from 0.5 to 2
- dress_first: bfloat16 [1024, 1024], replicated, may hold values from -0.1875 to 0.1875
- dress_second: bfloat16 [1024, 1024], replicated, may hold values from -0.1875 to 0.1875
Outputs:
- resid: bfloat16 [48, 512, 1024], P('col', None, 'row')
All inputs are finite; a program needn't handle non-finite values.
Results may differ from a plain program's by a relative error of at most 0.0061.
Values may be sent and summed in bfloat16 or wider, within the bound.
No kernel may reach another device: no remote copies, remote signals or barrier semaphores. Data moves between devices by JAX's collectives and lax.ppermute only.
A program may use at most 192 MiB of HBM per device.

v0:
```python
import jax
import jax.numpy as jnp
from jax import lax
from jax.sharding import PartitionSpec as P


def local(
    chol_window,
    chol_pairs,
    amplitudes,
    eps_window,
    eps_virtual,
    eps_occupied,
    dress_first,
    dress_second,
):
    window = lax.all_gather(chol_window, ("row", "col"), axis=2, tiled=True)
    block_b, block_d, aux_count = chol_pairs.shape
    window_size = window.shape[0]
    groups = window_size // 8
    window_blocks = window.reshape(groups, 8, window_size, aux_count)

    def build_tile(block_index):
        slab = lax.dynamic_index_in_dim(window_blocks, block_index, 0, keepdims=False)
        values = jnp.einsum("acq,bdq->abcd", slab, chol_pairs, preferred_element_type=jnp.float32)
        return values.astype(jnp.bfloat16)

    integrals = lax.map(build_tile, jnp.arange(groups, dtype=jnp.int32))
    integrals = integrals.reshape(window_size, block_b, window_size, block_d)
    partial_value = jnp.einsum(
        "abcd,cdo->abo",
        integrals,
        lax.all_gather(amplitudes, "row", axis=2, tiled=True),
        preferred_element_type=jnp.float32,
    )
    summed = lax.psum_scatter(partial_value, "col", scatter_dimension=0, tiled=True)
    rows_a = summed.shape[0]
    occ_count = summed.shape[2]
    denominator = (
        eps_window[:, None, None] + eps_virtual[None, :, None] + eps_occupied[None, None, :]
    )
    scaled = (summed / denominator).astype(jnp.bfloat16)
    flattened = scaled.reshape(rows_a * block_b, occ_count)
    first_mix = jnp.dot(flattened, dress_first, preferred_element_type=jnp.float32).astype(
        jnp.bfloat16
    )
    mixed = flattened.astype(jnp.float32) + jnp.dot(
        first_mix, dress_second, preferred_element_type=jnp.float32
    )
    mixed = mixed.astype(jnp.bfloat16).reshape(rows_a, block_b, occ_count)
    return lax.all_to_all(mixed, "row", split_axis=2, concat_axis=1, tiled=True)


def solution(mesh):
    return jax.shard_map(
        local,
        mesh=mesh,
        in_specs=(
            P(None, None, ("row", "col")),
            P("row", "col", None),
            P(None, "col", "row"),
            P("col"),
            P("row"),
            P(),
            P(),
            P(),
        ),
        out_specs=P("col", None, "row"),
        check_vma=False,
    )
```

profile of v0, /device:TPU:1, one launch (start us, length us, event | category | flops | bytes accessed | tf_op | source)
XLA Modules:
  0.0 322.5 jit_solution(2280201207964700690)
XLA Ops:
  6.5 0.7 all-gather.3.cloned.1.call-update
  7.3 0.0 all-gather.5.cloned.1.call-start
  7.3 1.9 copy.15
  9.2 0.0 reduce-scatter.4.cloned.1.call-start
  9.3 8.9 %copy.14 = bf16[64,32,1536]{2,0,1:T(8,128)(2,1)} copy(bf16[64,32,1536]{2,1,0:T(8,128)(2,1)} %param.11) | data formatting | bytes 12582912 | tf_op jit(solution)/shard_map/while | solution.py:28
  18.2 78.6 %all-gather.3.cloned.1.call-done = bf16[48,48,1536]{1,0,2:T(8,128)(2,1)} async-done(((bf16[48,48,12]{1,0,2:T(8,128)(2,1)}), bf16[48,48,1536]{1,0,2:T(8,128)(2,1)}) %all-gather.3.cloned.1.call-update) | async-done | bytes 7077904 | tf_op jit(solution)/shard_map/all_gather | solution.py:17
  96.8 20.1 %copy.13 = bf16[6,8,48,1536]{3,2,1,0:T(8,128)(2,1)} copy(bf16[6,8,48,1536]{2,1,0,3:T(8,128)(2,1)} %bitcast.46) | data formatting | bytes 14155776 | tf_op jit(solution)/shard_map/while | solution.py:28
  116.9 65.8 %while.10 = (s32[]{:T(128)}, bf16[6,8,64,48,32]{2,3,4,1,0:T(8,128)(2,1)}, s32[6]{0:T(128)S(1)}, bf16[6,8,48,1536]{3,2,1,0:T(8,128)(2,1)}, bf16[64,32,1536]{2,0,1...) while((s32[]{:T(128)}, bf16[6,8,64,48,32]{2,3,4,1,0:T(8,128)(2,1)}, s32[6]{0:T(128)S(1)}, ...), condition=%wide.region_1.2_spmd, body=%wide.region_0.1_spmd.sunk | while | flops 2416705536 | bytes 10617479 | solution.py:28
  116.9 0.6 dynamic_slice.15
  119.2 8.6 %bitcast_dynamic-update-slice_fusion.2 = bf16[6,8,64,48,32]{2,3,4,1,0:T(8,128)(2,1)} fusion(bf16[6,8,64,48,32]{2,3,4,1,0:T(8,128)(2,1)} %get-tuple-element.93, s32[]{:T(128)} %get-tuple-element.92, bf16[64,32,1536]{2,0,1:T(8,128)(2,1)} %get-tuple-element.104, bf16[6,8,48,1536]{3,2,1,0:T(8,128)(2,1)} %get-tuple-element.103, s32[]{:T(128)S(6)} %select_n.5), kind=kOutput, calls=%fused_computation.2.clone.1 | convolution fusion | flops 2416705536 | bytes 10617348 | tf_op jit(solution)/shard_map/while/body/eval_jaxpr/acq,bdq->abcd/dot_general | solution.py:25
  127.8 0.6 dynamic_slice.15
  130.1 8.6 %bitcast_dynamic-update-slice_fusion.2 = bf16[6,8,64,48,32]{2,3,4,1,0:T(8,128)(2,1)} fusion(bf16[6,8,64,48,32]{2,3,4,1,0:T(8,128)(2,1)} %get-tuple-element.93, s32[]{:T(128)} %get-tuple-element.92, bf16[64,32,1536]{2,0,1:T(8,128)(2,1)} %get-tuple-element.104, bf16[6,8,48,1536]{3,2,1,0:T(8,128)(2,1)} %get-tuple-element.103, s32[]{:T(128)S(6)} %select_n.5), kind=kOutput, calls=%fused_computation.2.clone.1 | convolution fusion | flops 2416705536 | bytes 10617348 | tf_op jit(solution)/shard_map/while/body/eval_jaxpr/acq,bdq->abcd/dot_general | solution.py:25
  138.8 0.6 dynamic_slice.15
  141.1 8.6 %bitcast_dynamic-update-slice_fusion.2 = bf16[6,8,64,48,32]{2,3,4,1,0:T(8,128)(2,1)} fusion(bf16[6,8,64,48,32]{2,3,4,1,0:T(8,128)(2,1)} %get-tuple-element.93, s32[]{:T(128)} %get-tuple-element.92, bf16[64,32,1536]{2,0,1:T(8,128)(2,1)} %get-tuple-element.104, bf16[6,8,48,1536]{3,2,1,0:T(8,128)(2,1)} %get-tuple-element.103, s32[]{:T(128)S(6)} %select_n.5), kind=kOutput, calls=%fused_computation.2.clone.1 | convolution fusion | flops 2416705536 | bytes 10617348 | tf_op jit(solution)/shard_map/while/body/eval_jaxpr/acq,bdq->abcd/dot_general | solution.py:25
  149.7 0.6 dynamic_slice.15
  152.0 8.7 %bitcast_dynamic-update-slice_fusion.2 = bf16[6,8,64,48,32]{2,3,4,1,0:T(8,128)(2,1)} fusion(bf16[6,8,64,48,32]{2,3,4,1,0:T(8,128)(2,1)} %get-tuple-element.93, s32[]{:T(128)} %get-tuple-element.92, bf16[64,32,1536]{2,0,1:T(8,128)(2,1)} %get-tuple-element.104, bf16[6,8,48,1536]{3,2,1,0:T(8,128)(2,1)} %get-tuple-element.103, s32[]{:T(128)S(6)} %select_n.5), kind=kOutput, calls=%fused_computation.2.clone.1 | convolution fusion | flops 2416705536 | bytes 10617348 | tf_op jit(solution)/shard_map/while/body/eval_jaxpr/acq,bdq->abcd/dot_general | solution.py:25
  160.7 0.6 dynamic_slice.15
  163.0 8.7 %bitcast_dynamic-update-slice_fusion.2 = bf16[6,8,64,48,32]{2,3,4,1,0:T(8,128)(2,1)} fusion(bf16[6,8,64,48,32]{2,3,4,1,0:T(8,128)(2,1)} %get-tuple-element.93, s32[]{:T(128)} %get-tuple-element.92, bf16[64,32,1536]{2,0,1:T(8,128)(2,1)} %get-tuple-element.104, bf16[6,8,48,1536]{3,2,1,0:T(8,128)(2,1)} %get-tuple-element.103, s32[]{:T(128)S(6)} %select_n.5), kind=kOutput, calls=%fused_computation.2.clone.1 | convolution fusion | flops 2416705536 | bytes 10617348 | tf_op jit(solution)/shard_map/while/body/eval_jaxpr/acq,bdq->abcd/dot_general | solution.py:25
  171.7 0.6 dynamic_slice.15
  174.0 8.7 %bitcast_dynamic-update-slice_fusion.2 = bf16[6,8,64,48,32]{2,3,4,1,0:T(8,128)(2,1)} fusion(bf16[6,8,64,48,32]{2,3,4,1,0:T(8,128)(2,1)} %get-tuple-element.93, s32[]{:T(128)} %get-tuple-element.92, bf16[64,32,1536]{2,0,1:T(8,128)(2,1)} %get-tuple-element.104, bf16[6,8,48,1536]{3,2,1,0:T(8,128)(2,1)} %get-tuple-element.103, s32[]{:T(128)S(6)} %select_n.5), kind=kOutput, calls=%fused_computation.2.clone.1 | convolution fusion | flops 2416705536 | bytes 10617348 | tf_op jit(solution)/shard_map/while/body/eval_jaxpr/acq,bdq->abcd/dot_general | solution.py:25
  182.7 17.6 %convolution_bitcast_fusion = f32[48,64,1024]{2,1,0:T(8,128)} fusion(bf16[48,64,48,32]{1,2,3,0:T(8,128)(2,1)} %bitcast.45, bf16[48,32,1024]{2,0,1:T(8,128)(2,1)} %all-gather.5.cloned.1.call-done), kind=kOutput, calls=%fused_computation.6 | convolution fusion | flops 9663676416 | bytes 25165824 | tf_op jit(solution)/shard_map/abcd,cdo->abo/dot_general | solution.py:30
  200.3 0.0 reduce-scatter.4.cloned.1.call-update
  200.4 0.6 copy-done.2
  201.0 0.1 broadcast_add_fusion
  201.1 93.2 %reduce-scatter.4.cloned.1.call-done = f32[3,64,1024]{2,1,0:T(8,128)} async-done(((f32[48,64,1024]{2,1,0:T(8,128)}), f32[3,64,1024]{2,1,0:T(8,128)}) %reduce-scatter.4.cloned.1.call-update) | async-done | bytes 786448
  294.3 1.3 divide_convert_fusion
  295.6 2.6 fusion.8
  298.2 0.7 copy.16
  298.9 0.7 reshape.54
  299.7 13.4 %all_to_all.18 = bf16[8,2,12288]{2,1,0:T(2,128)(2,1)} all-to-all(bf16[8,2,12288]{2,1,0:T(2,128)(2,1)S(1)} %reshape.54), channel_id=1, replica_groups=mesh['row'=8,'col'=16] {'row'}, dimensions={0} | all-to-all | bytes 786432 | tf_op jit(solution)/shard_map/all_to_all | solution.py:51
  313.1 1.6 reshape.55
  314.7 1.2 copy.17
  (12 shorter events, 0.0 us)
Async XLA Ops:
  6.5 289.1 %copy-start = (bf16[1024,1024]{1,0:T(8,128)(2,1)S(1)}, bf16[1024,1024]{1,0:T(8,128)(2,1)}, u32[]{:S(2)}) copy-start(bf16[1024,1024]{1,0:T(8,128)(2,1)} %param.17) | copy-start | bytes 6291460
  6.5 90.3 %all-gather.3.cloned.1.call-start = ((), (), s32[]{:S(2)}) async-start(), calls=%async_computation.2 | async-start | bytes 19021824 | tf_op jit(solution)/shard_map/all_gather | solution.py:17
  7.3 175.4 %all-gather.5.cloned.1.call-start = ((), (), s32[]{:S(2)}) async-start(), calls=%async_computation.3 | async-start | bytes 3538944 | tf_op jit(solution)/shard_map/all_gather | solution.py:33
  9.2 285.1 %reduce-scatter.4.cloned.1.call-start = ((), (), s32[]{:S(2)}) async-start(), calls=%async_computation.4 | async-start | bytes 13369344
  200.3 0.7 copy-start.2
  200.3 0.7 copy-start.3
  200.3 94.0 %copy-start.1 = (f32[1024]{0:T(1024)S(1)}, f32[1024]{0:T(1024)}, u32[]{:S(2)}) copy-start(f32[1024]{0:T(1024)} %param.15) | copy-start | bytes 12292
Sparse Core Ops, SparseCore 0:
  10.2 86.5 all-gather.2
  98.5 30.5 all-gather.4
  200.5 93.7 reduce-scatter.3
where the time goes:
time: 323 us; the launch traced here: 322 us
  waiting for transfers between devices  173 us (54%)
  matrix products  72.1 us (22%)
  local copies, waits for them, and re-layouts  39.3 us (12%)
  blocking collectives  13.4 us (4%)
  between operations  13.2 us (4%)
  loops' own time  10.4 us (3%)
    unnamed x4, waiting for transfers between devices  94 us
    all_gather x1, waiting for transfers between devices, local(): window = lax.all_gather(chol_window, ('row', 'col'), axis=2, tiled=True)  78.6 us
    dot_general x6, matrix products, build_tile(): jnp.einsum('acq,bdq->abcd', slab, chol_pairs, preferred_element_type=jnp....  51.9 us
    while x2, local copies, waits for them, and re-layouts, local(): integrals = lax.map(build_tile, jnp.arange(groups, dtype=jnp.int32))  29 us
    dot_general x1, matrix products, local(): jnp.einsum('abcd,cdo->abo', integrals, lax.all_gather(amplitudes, 'row',...  17.6 us
    all_to_all x1, blocking collectives, local(): return lax.all_to_all(mixed, 'row', split_axis=2, concat_axis=1, tiled=True)  13.4 us
    another operation x1, loops' own time, local(): integrals = lax.map(build_tile, jnp.arange(groups, dtype=jnp.int32))  10.4 us
  transfers between devices with their start and end apart: 3, of which 2 were waited for; matrix products, arithmetic and copies ran while one was open for 27% of the time, Pallas kernels for 0%

commit v1 on v0

--- a/solution.py
+++ b/solution.py
@@ -14,7 +14,8 @@
     dress_first,
     dress_second,
 ):
-    window = lax.all_gather(chol_window, ("row", "col"), axis=2, tiled=True)
+    outgoing = jnp.stack([chol_window] * lax.axis_size(("row", "col")))
+    window = jnp.concatenate(lax.all_to_all(outgoing, ("row", "col"), 0, 0), axis=2)
     block_b, block_d, aux_count = chol_pairs.shape
     window_size = window.shape[0]
     groups = window_size // 8

time: 323 us -> 411 us (1.27)
  local copies, waits for them, and re-layouts: 39.3 us -> 113 us
  starting transfers between devices: 0.08 us -> 12 us
    all_to_all x0 -> x1, waiting for transfers between devices: none -> 79.1 us  [local(): lax.all_to_all(outgoing, ('row', 'col'), 0, 0)]
    all_gather x1 -> x0, waiting for transfers between devices: 78.6 us -> none  [local(): window = lax.all_gather(chol_window, ('row', 'col'), axis=2, tiled=True)]
    unnamed x11 -> x16, local copies, waits for them, and re-layouts: 4.91 us -> 78.5 us
    all_to_all x0 -> x1, starting transfers between devices: none -> 11.9 us  [local(): lax.all_to_all(outgoing, ('row', 'col'), 0, 0)]
    unnamed x4 -> x3, waiting for transfers between devices: 94 us -> 94.8 us
  transfers between devices with their start and end apart: 3 -> 3, of which waited for: 2 -> 2; matrix products, arithmetic and copies ran while one was open for 27% -> 28% of each run, Pallas kernels for 0% -> 0%
where the time goes in v1:
time: 411 us; the launch traced here: 409 us
  waiting for transfers between devices  174 us (42%)
  local copies, waits for them, and re-layouts  113 us (27%)
  matrix products  72.1 us (18%)
  between operations  13.5 us (3%)
  blocking collectives  13.4 us (3%)
  starting transfers between devices  12 us (3%)
  loops' own time  10.4 us (3%)
    unnamed x3, waiting for transfers between devices  94.8 us
    all_to_all x1, waiting for transfers between devices, local(): lax.all_to_all(outgoing, ('row', 'col'), 0, 0)  79.1 us
    unnamed x16, local copies, waits for them, and re-layouts  78.5 us
    dot_general x6, matrix products, build_tile(): jnp.einsum('acq,bdq->abcd', slab, chol_pairs, preferred_element_type=jnp....  51.9 us
    while x2, local copies, waits for them, and re-layouts, local(): integrals = lax.map(build_tile, jnp.arange(groups, dtype=jnp.int32))  28.9 us
    dot_general x1, matrix products, local(): jnp.einsum('abcd,cdo->abo', integrals, lax.all_gather(amplitudes, 'row',...  17.6 us
    all_to_all x1, blocking collectives, local(): return lax.all_to_all(mixed, 'row', split_axis=2, concat_axis=1, tiled=True)  13.4 us
    all_to_all x1, starting transfers between devices, local(): lax.all_to_all(outgoing, ('row', 'col'), 0, 0)  11.9 us
  transfers between devices with their start and end apart: 3, of which 2 were waited for; matrix products, arithmetic and copies ran while one was open for 28% of the time, Pallas kernels for 0%

profile of v1, /device:TPU:1, one launch (start us, length us, event | category | flops | bytes accessed | tf_op | source)
XLA Modules:
  0.0 409.5 jit_solution(11297862932125010521)
XLA Ops:
  6.5 8.2 %broadcast_bitcast_fusion = bf16[128,12,48,48]{3,2,1,0:T(8,128)(2,1)} fusion(bf16[48,48,12]{1,0,2:T(8,128)(2,1)} %param.10), kind=kLoop, calls=%fused_computation.13 | loop fusion | bytes 7133184
  14.7 38.3 %reshape.56 = bf16[128,2,13824]{2,1,0:T(2,128)(2,1)} reshape(bf16[128,12,48,48]{3,2,1,0:T(8,128)(2,1)} %broadcast_bitcast_fusion) | data formatting | bytes 14155776
  53.0 11.9 %all-to-all-start = ((bf16[128,2,13824]{2,1,0:T(2,128)(2,1)}), bf16[128,2,13824]{2,1,0:T(2,128)(2,1)}, u32[]{:S(2)}, u32[]{:S(2)}) async-start(bf16[128,2,13824]{2,1,0:T(2,128)(2,1)} %reshape.56), calls=%async_computation | async-start | bytes 14155776 | tf_op jit(solution)/shard_map/all_to_all | solution.py:18
  65.0 0.9 copy.19
  65.9 8.9 %copy.18 = bf16[64,32,1536]{2,0,1:T(8,128)(2,1)} copy(bf16[64,32,1536]{2,1,0:T(8,128)(2,1)} %param.11) | data formatting | bytes 12582912 | tf_op jit(solution)/shard_map/while | solution.py:29
  74.8 79.1 %all-to-all-done = bf16[128,2,13824]{2,1,0:T(2,128)(2,1)} async-done(((bf16[128,2,13824]{2,1,0:T(2,128)(2,1)}), bf16[128,2,13824]{2,1,0:T(2,128)(2,1)}, u32[]{:S(2)}, u32[]{:S(2)}) %all-to-all-start) | async-done | bytes 7077920 | tf_op jit(solution)/shard_map/all_to_all | solution.py:18
  153.9 28.1 %reshape.57 = bf16[128,12,48,48]{3,2,1,0:T(8,128)(2,1)} reshape(bf16[128,2,13824]{2,1,0:T(2,128)(2,1)} %all-to-all-done) | data formatting | bytes 14155776
  182.1 20.0 %copy.17 = bf16[6,8,48,1536]{3,2,1,0:T(8,128)(2,1)} copy(bf16[6,8,48,1536]{2,1,0,3:T(8,128)(2,1)} %bitcast.50) | data formatting | bytes 14155776 | tf_op jit(solution)/shard_map/while | solution.py:29
  202.0 65.8 %while.10 = (s32[]{:T(128)}, bf16[6,8,64,48,32]{2,3,4,1,0:T(8,128)(2,1)}, s32[6]{0:T(128)S(1)}, bf16[6,8,48,1536]{3,2,1,0:T(8,128)(2,1)}, bf16[64,32,1536]{2,0,1...) while((s32[]{:T(128)}, bf16[6,8,64,48,32]{2,3,4,1,0:T(8,128)(2,1)}, s32[6]{0:T(128)S(1)}, ...), condition=%wide.region_1.2_spmd, body=%wide.region_0.1_spmd.sunk | while | flops 2416705536 | bytes 10617479 | solution.py:29
  202.0 0.6 dynamic_slice.15
  204.4 8.6 %bitcast_dynamic-update-slice_fusion.2 = bf16[6,8,64,48,32]{2,3,4,1,0:T(8,128)(2,1)} fusion(bf16[6,8,64,48,32]{2,3,4,1,0:T(8,128)(2,1)} %get-tuple-element.98, s32[]{:T(128)} %get-tuple-element.97, bf16[64,32,1536]{2,0,1:T(8,128)(2,1)} %get-tuple-element.109, bf16[6,8,48,1536]{3,2,1,0:T(8,128)(2,1)} %get-tuple-element.108, s32[]{:T(128)S(6)} %select_n.5), kind=kOutput, calls=%fused_computation.2.clone.1 | convolution fusion | flops 2416705536 | bytes 10617348 | tf_op jit(solution)/shard_map/while/body/eval_jaxpr/acq,bdq->abcd/dot_general | solution.py:26
  213.0 0.6 dynamic_slice.15
  215.3 8.6 %bitcast_dynamic-update-slice_fusion.2 = bf16[6,8,64,48,32]{2,3,4,1,0:T(8,128)(2,1)} fusion(bf16[6,8,64,48,32]{2,3,4,1,0:T(8,128)(2,1)} %get-tuple-element.98, s32[]{:T(128)} %get-tuple-element.97, bf16[64,32,1536]{2,0,1:T(8,128)(2,1)} %get-tuple-element.109, bf16[6,8,48,1536]{3,2,1,0:T(8,128)(2,1)} %get-tuple-element.108, s32[]{:T(128)S(6)} %select_n.5), kind=kOutput, calls=%fused_computation.2.clone.1 | convolution fusion | flops 2416705536 | bytes 10617348 | tf_op jit(solution)/shard_map/while/body/eval_jaxpr/acq,bdq->abcd/dot_general | solution.py:26
  223.9 0.6 dynamic_slice.15
  226.3 8.6 %bitcast_dynamic-update-slice_fusion.2 = bf16[6,8,64,48,32]{2,3,4,1,0:T(8,128)(2,1)} fusion(bf16[6,8,64,48,32]{2,3,4,1,0:T(8,128)(2,1)} %get-tuple-element.98, s32[]{:T(128)} %get-tuple-element.97, bf16[64,32,1536]{2,0,1:T(8,128)(2,1)} %get-tuple-element.109, bf16[6,8,48,1536]{3,2,1,0:T(8,128)(2,1)} %get-tuple-element.108, s32[]{:T(128)S(6)} %select_n.5), kind=kOutput, calls=%fused_computation.2.clone.1 | convolution fusion | flops 2416705536 | bytes 10617348 | tf_op jit(solution)/shard_map/while/body/eval_jaxpr/acq,bdq->abcd/dot_general | solution.py:26
  234.9 0.6 dynamic_slice.15
  237.2 8.7 %bitcast_dynamic-update-slice_fusion.2 = bf16[6,8,64,48,32]{2,3,4,1,0:T(8,128)(2,1)} fusion(bf16[6,8,64,48,32]{2,3,4,1,0:T(8,128)(2,1)} %get-tuple-element.98, s32[]{:T(128)} %get-tuple-element.97, bf16[64,32,1536]{2,0,1:T(8,128)(2,1)} %get-tuple-element.109, bf16[6,8,48,1536]{3,2,1,0:T(8,128)(2,1)} %get-tuple-element.108, s32[]{:T(128)S(6)} %select_n.5), kind=kOutput, calls=%fused_computation.2.clone.1 | convolution fusion | flops 2416705536 | bytes 10617348 | tf_op jit(solution)/shard_map/while/body/eval_jaxpr/acq,bdq->abcd/dot_general | solution.py:26
  245.9 0.6 dynamic_slice.15
  248.2 8.7 %bitcast_dynamic-update-slice_fusion.2 = bf16[6,8,64,48,32]{2,3,4,1,0:T(8,128)(2,1)} fusion(bf16[6,8,64,48,32]{2,3,4,1,0:T(8,128)(2,1)} %get-tuple-element.98, s32[]{:T(128)} %get-tuple-element.97, bf16[64,32,1536]{2,0,1:T(8,128)(2,1)} %get-tuple-element.109, bf16[6,8,48,1536]{3,2,1,0:T(8,128)(2,1)} %get-tuple-element.108, s32[]{:T(128)S(6)} %select_n.5), kind=kOutput, calls=%fused_computation.2.clone.1 | convolution fusion | flops 2416705536 | bytes 10617348 | tf_op jit(solution)/shard_map/while/body/eval_jaxpr/acq,bdq->abcd/dot_general | solution.py:26
  256.8 0.6 dynamic_slice.15
  259.1 8.7 %bitcast_dynamic-update-slice_fusion.2 = bf16[6,8,64,48,32]{2,3,4,1,0:T(8,128)(2,1)} fusion(bf16[6,8,64,48,32]{2,3,4,1,0:T(8,128)(2,1)} %get-tuple-element.98, s32[]{:T(128)} %get-tuple-element.97, bf16[64,32,1536]{2,0,1:T(8,128)(2,1)} %get-tuple-element.109, bf16[6,8,48,1536]{3,2,1,0:T(8,128)(2,1)} %get-tuple-element.108, s32[]{:T(128)S(6)} %select_n.5), kind=kOutput, calls=%fused_computation.2.clone.1 | convolution fusion | flops 2416705536 | bytes 10617348 | tf_op jit(solution)/shard_map/while/body/eval_jaxpr/acq,bdq->abcd/dot_general | solution.py:26
  267.8 17.6 %convolution_bitcast_fusion = f32[48,64,1024]{2,1,0:T(8,128)} fusion(bf16[48,64,48,32]{1,2,3,0:T(8,128)(2,1)} %bitcast.51, bf16[48,32,1024]{2,0,1:T(8,128)(2,1)} %all-gather.2.cloned.1.call-done), kind=kOutput, calls=%fused_computation.6 | convolution fusion | flops 9663676416 | bytes 25165824 | tf_op jit(solution)/shard_map/abcd,cdo->abo/dot_general | solution.py:31
  285.5 0.6 copy-done.3
  286.2 0.1 broadcast_add_fusion
  286.2 94.8 %reduce-scatter.4.cloned.1.call-done = f32[3,64,1024]{2,1,0:T(8,128)} async-done(((f32[48,64,1024]{2,1,0:T(8,128)}), f32[3,64,1024]{2,1,0:T(8,128)}) %reduce-scatter.4.cloned.1.call-update) | async-done | bytes 786448
  381.0 1.3 divide_convert_fusion
  382.3 2.6 fusion.8
  384.9 0.7 copy.20
  385.6 0.7 reshape.58
  386.4 13.4 %all_to_all.23 = bf16[8,2,12288]{2,1,0:T(2,128)(2,1)} all-to-all(bf16[8,2,12288]{2,1,0:T(2,128)(2,1)S(1)} %reshape.58), channel_id=1, replica_groups=mesh['row'=8,'col'=16] {'row'}, dimensions={0} | all-to-all | bytes 786432 | tf_op jit(solution)/shard_map/all_to_all | solution.py:52
  399.8 1.6 reshape.59
  401.4 1.2 copy.21
  (16 shorter events, 0.2 us)
Async XLA Ops:
  6.5 375.8 %copy-start = (bf16[1024,1024]{1,0:T(8,128)(2,1)S(1)}, bf16[1024,1024]{1,0:T(8,128)(2,1)}, u32[]{:S(2)}) copy-start(bf16[1024,1024]{1,0:T(8,128)(2,1)} %param.17) | copy-start | bytes 6291460
  53.0 11.9 %copy-start.1 = (bf16[48,32,128]{2,1,0:T(8,128)(2,1)S(1)}, bf16[48,32,128]{2,1,0:T(8,128)(2,1)}, u32[]{:S(2)}) copy-start(bf16[48,32,128]{2,1,0:T(8,128)(2,1)} %param.12) | copy-start | bytes 1179652
  53.0 100.9 %all-to-all-start = ((bf16[128,2,13824]{2,1,0:T(2,128)(2,1)}), bf16[128,2,13824]{2,1,0:T(2,128)(2,1)}, u32[]{:S(2)}, u32[]{:S(2)}) async-start(bf16[128,2,13824]{2,1,0:T(2,128)(2,1)} %reshape.56), calls=%async_computation | async-start | bytes 14155776 | tf_op jit(solution)/shard_map/all_to_all | solution.py:18
  64.9 202.9 %all-gather.2.cloned.1.call-start = ((), (), s32[]{:S(2)}) async-start(), calls=%async_computation.3 | async-start | bytes 3538944 | tf_op jit(solution)/shard_map/all_gather | solution.py:34
  65.9 315.1 %reduce-scatter.4.cloned.1.call-start = ((), (), s32[]{:S(2)}) async-start(), calls=%async_computation.4 | async-start | bytes 13369344
  285.5 0.7 copy-start.3
  285.5 0.7 copy-start.4
  285.5 95.5 %copy-start.2 = (f32[1024]{0:T(1024)S(1)}, f32[1024]{0:T(1024)}, u32[]{:S(2)}) copy-start(f32[1024]{0:T(1024)} %param.15) | copy-start | bytes 12292
Sparse Core Ops, SparseCore 0:
  67.4 93.0 all-gather.1
  285.6 95.3 reduce-scatter.3
